TPU v7x, 256 devices: a whole 4x4x8 slice. The times are simulated.
256 devices in a mesh: grp: 16 (over z, core), pts: 16 (over y, x).
Axes of the slice: x: 4, y: 4, z: 8, core: 2. Of those that a mesh axis runs over, the one named last changes fastest.
Arguments:
- patches: bfloat16 [16, 16, 16384, 128], P('grp', 'pts'), may hold values from -6 to 6
- counts: int32 [16, 16], replicated, may hold values from 1 to 16384, as said below
- pick_slot: int32 [3, 128], replicated, may hold values from 0 to 16383, as said below
- block_owner: int32 [3], replicated, may hold values from 0 to 255, as said below
Outputs:
- factor_rows: bfloat16 [16, 16, 8192, 384], P('grp', 'pts')
- residual_gain: float32 [16, 16, 8192], P('grp', 'pts')
Inputs may be any that keep to these rules, and one draw needn't show every extreme that they name: `counts`: each row sums to 131072, and in every row one device holds exactly 16384; in the last row it is the last column. `pick_slot`: the 128 slots of round r are distinct and below the count of block_owner[r]; the round owned by the last device includes slot 16383. `block_owner`: the owners of the rounds are distinct devices, and one of them is the last device.
All inputs are finite; a program needn't handle non-finite values.
Results may differ from a plain program's by a relative error of at most 0.0075.
Values may be sent and summed in bfloat16 or wider, within the bound.
A program may use at most 192 MiB of HBM per device.

v0:
```python
import jax
import jax.numpy as jnp
from jax import lax
from jax.sharding import PartitionSpec as P

PTS_DEV = 8192
JITTER = 0.1
HIGHEST = lax.Precision.HIGHEST


def from_root(block, axis, holder):
    block = jnp.where(lax.axis_index(axis) == holder, block, jnp.zeros_like(block))
    return lax.psum(block, axis)


def squares(matrix):
    return jnp.sum(jnp.square(matrix.astype(jnp.float32)), axis=1)


def affinity(row_data, rows_sq, row_ids, block_rows, block_sq, block_ids):
    cross_dot = lax.dot_general(
        row_data, block_rows, (((1,), (1,)), ((), ())), preferred_element_type=jnp.float32
    )
    inverse_scale = 1.0 / row_data.shape[1]
    distance = rows_sq[:, None] + block_sq[None, :] - 2.0 * cross_dot
    same_point = (row_ids[:, None] == block_ids[None, :]).astype(jnp.float32)
    return jnp.exp(-inverse_scale * distance) + JITTER * same_point


def extend(factors, kernel_part, cross_rows, inverse):
    if factors.shape[1] > 0:
        kernel_part = kernel_part - lax.dot_general(
            factors,
            cross_rows,
            (((1,), (1,)), ((), ())),
            precision=HIGHEST,
            preferred_element_type=jnp.float32,
        )
    fresh_rows = lax.dot_general(
        kernel_part,
        inverse,
        (((1,), (1,)), ((), ())),
        precision=HIGHEST,
        preferred_element_type=jnp.float32,
    )
    return jnp.concatenate([factors, fresh_rows], axis=1)


def prepare(blocks, block_ids):
    round_count, block_size = block_ids.shape
    stacked = blocks.reshape(round_count * block_size, blocks.shape[2])
    stacked_ids = block_ids.reshape(-1)
    stacked_sq = squares(stacked)
    factors = jnp.zeros((round_count * block_size, 0), jnp.float32)
    identity = jnp.eye(block_size, dtype=jnp.float32)
    inverses = []
    crosses = []
    for step_index in range(round_count):
        lower_edge = step_index * block_size
        cross_rows = factors[lower_edge : lower_edge + block_size]
        block_sq = stacked_sq[lower_edge : lower_edge + block_size]
        schur_block = affinity(
            blocks[step_index],
            block_sq,
            block_ids[step_index],
            blocks[step_index],
            block_sq,
            block_ids[step_index],
        )
        if step_index > 0:
            schur_block = schur_block - lax.dot_general(
                cross_rows,
                cross_rows,
                (((1,), (1,)), ((), ())),
                precision=HIGHEST,
                preferred_element_type=jnp.float32,
            )
        factor_low = jnp.linalg.cholesky(schur_block)
        inverse = lax.linalg.triangular_solve(factor_low, identity, left_side=True, lower=True)
        kernel_part = affinity(
            stacked, stacked_sq, stacked_ids, blocks[step_index], block_sq, block_ids[step_index]
        )
        factors = extend(factors, kernel_part, cross_rows, inverse)
        inverses.append(inverse)
        crosses.append(cross_rows)
    return (inverses, crosses)


def factorize(row_data, row_ids, blocks, block_ids, inverses, crosses):
    rows_sq = squares(row_data)
    blocks_sq = squares(blocks.reshape(-1, blocks.shape[2])).reshape(block_ids.shape)
    factors = jnp.zeros((row_data.shape[0], 0), jnp.float32)
    for step_index in range(len(inverses)):
        kernel_part = affinity(
            row_data,
            rows_sq,
            row_ids,
            blocks[step_index],
            blocks_sq[step_index],
            block_ids[step_index],
        )
        factors = extend(factors, kernel_part, crosses[step_index], inverses[step_index])
    point_gains = 1.0 + JITTER - jnp.sum(factors * factors, axis=1)
    return (factors, point_gains)


def per_device(patches, counts, pick_slot, block_owner):
    groups = lax.axis_size("grp")
    columns = lax.axis_size("pts")
    my_group = lax.axis_index("grp")
    my_column = lax.axis_index("pts")
    local_rows = patches[0, 0]
    slot_count = local_rows.shape[0]
    embed_width = local_rows.shape[1]
    per_peer = slot_count // groups
    round_count, block_size = pick_slot.shape
    ends_table = jnp.cumsum(counts, axis=1)
    starts_table = ends_table - counts
    col_ends = lax.dynamic_index_in_dim(ends_table, my_column, 0, keepdims=False)
    col_starts = lax.dynamic_index_in_dim(starts_table, my_column, 0, keepdims=False)
    my_start = lax.dynamic_index_in_dim(col_starts, my_group, 0, keepdims=False)
    my_count = lax.dynamic_index_in_dim(col_ends, my_group, 0, keepdims=False) - my_start
    target = jnp.arange(groups, dtype=jnp.int32)[:, None]
    offsets = (target - my_start) % groups + jnp.arange(per_peer, dtype=jnp.int32)[None, :] * groups
    in_range = offsets < my_count
    take_rows = jnp.minimum(offsets, slot_count - 1).reshape(-1)
    slot_rank = jnp.arange(PTS_DEV, dtype=jnp.int32) * groups + my_group
    sources = jnp.sum((col_ends[None, :] <= slot_rank[:, None]).astype(jnp.int32), axis=1)
    begin_slot = (col_starts + (my_group - col_starts) % groups) // groups
    source_hit = jnp.arange(groups, dtype=jnp.int32)[None, :] == sources[:, None]
    source_begin = jnp.sum(jnp.where(source_hit, begin_slot[None, :], 0), axis=1)
    take_index = sources * per_peer + jnp.arange(PTS_DEV, dtype=jnp.int32) - source_begin
    owner_group = block_owner // columns
    owner_column = block_owner % columns
    pick_rank = starts_table[owner_column, owner_group][:, None] + pick_slot
    block_ids = (
        pick_rank % groups * columns + owner_column[:, None]
    ) * PTS_DEV + pick_rank // groups
    chosen = jnp.take(local_rows, pick_slot.reshape(-1), axis=0).reshape(
        round_count, block_size, embed_width
    )
    fetched = []
    for step_index in range(round_count):
        fetched.append(from_root(chosen[step_index], ("grp", "pts"), block_owner[step_index]))
    blocks = jnp.stack(fetched)
    inverses, crosses = prepare(blocks, block_ids)
    shaped = jnp.take(local_rows, take_rows, axis=0).reshape(
        (groups, per_peer) + local_rows.shape[1:]
    )
    keep_mask = in_range.reshape((groups, per_peer) + (1,) * (local_rows.ndim - 1))
    received = lax.all_to_all(
        jnp.where(keep_mask, shaped, jnp.zeros((), local_rows.dtype)),
        "grp",
        split_axis=0,
        concat_axis=0,
        tiled=True,
    )
    flat_rows = received.reshape((groups * per_peer,) + received.shape[2:])
    points = jnp.take(flat_rows, take_index, axis=0)
    point_ids = (my_group * columns + my_column) * PTS_DEV + jnp.arange(PTS_DEV, dtype=jnp.int32)
    factors, point_gains = factorize(points, point_ids, blocks, block_ids, inverses, crosses)
    factor_rows = factors.astype(jnp.bfloat16)
    return (factor_rows[None, None], point_gains[None, None])


def solution(mesh):
    in_specs = (P("grp", "pts", None, None), P(), P(), P())
    out_specs = (P("grp", "pts", None, None), P("grp", "pts", None))
    return jax.shard_map(
        per_device, mesh=mesh, in_specs=in_specs, out_specs=out_specs, check_vma=False
    )
```

profile of v0, /device:TPU:1, one launch (start us, length us, event | category | flops | bytes accessed | tf_op | source)
XLA Modules:
  0.0 556.6 jit_solution(17895677158123767266)
XLA Ops:
  7.2 0.9 reduce_window_sum.11
  8.0 0.7 sub.107
  12.2 58.2 %gather_fusion = bf16[16384,128]{1,0:T(8,128)(2,1)} fusion(bf16[16384,128]{1,0:T(8,128)(2,1)} %bitcast.108, s32[16384]{0:T(1024)S(1)} %broadcast_clamp_fusion), kind=kCustom, calls=%fused_computation | custom fusion | bytes 8454144 | tf_op jit(solution)/shard_map/jit(_take)/gather | solution.py:147
  70.4 7.6 %select_select_fusion = bf16[16,1024,128]{2,1,0:T(8,128)(2,1)} fusion(bf16[16,1024,128]{2,1,0:T(8,128)(2,1)} %bitcast.110, pred[16,1024]{1,0:T(8,128)(4,1)S(1)} %get-tuple-element.21, pred[16,1024]{1,0:T(8,128)(4,1)S(1)} %get-tuple-element.20), kind=kLoop, calls=%fused_computation.28 | loop fusion | flops 4194304 | bytes 8421376 | tf_op jit(solution)/shard_map/jit(_where)/select_n | solution.py:152
  78.0 10.1 %all-to-all-start = ((bf16[16,1024,128]{2,1,0:T(8,128)(2,1)}), bf16[16,1024,128]{2,1,0:T(8,128)(2,1)}, u32[]{:S(2)}, u32[]{:S(2)}) async-start(bf16[16,1024,128]{2,1,0:T(8,128)(2,1)} %select_select_fusion), calls=%async_computation | async-start | bytes 8388608 | tf_op jit(solution)/shard_map/all_to_all | solution.py:151
  90.8 4.2 gather_fusion.2
  97.1 284.2 %all-reduce.3.cloned.1.call-done = (bf16[128,128]{1,0:T(8,128)(2,1)}, bf16[128,128]{1,0:T(8,128)(2,1)}, bf16[128,128]{1,0:T(8,128)(2,1)}) async-done(((bf16[128,128]{1,0:T(8,128)(2,1)}, bf16[128,128]{1,0:T(8,128)(2,1)}, bf16[128,128]{1,0:T(8,128)(2,1)}), (bf16[128,128]{1,0:T(8,128)(2,1)}, bf16[128,128]{1,0:T(8,128)(2,1)}, bf16[128,128]{1,0:T(8,128)(2,1)})) %all-reduce.3.cloned.1.call-update) | async-done | bytes 98320 | tf_op jit(solution)/shard_map/psum | solution.py:13
  381.4 0.9 multiply_reduce_fusion.1
  382.3 1.0 fusion.36
  383.5 11.7 %cholesky.59 = f32[128,128]{1,0:T(8,128)S(1)} custom-call(f32[128,128]{1,0:T(8,128)S(1)} %fusion.54), custom_call_target="Cholesky" | custom-call | tf_op jit(solution)/shard_map/jit(cholesky)/cholesky | solution.py:78
  396.5 9.8 %custom-call.9 = f32[1,128,128]{1,2,0:T(8,128)S(1)} custom-call(f32[1,128,128]{2,1,0:T(8,128)S(1)} %fusion.46), custom_call_target="InvertDiagBlocksLowerTriangular" | custom-call | tf_op jit(solution)/shard_map/triangular_solve/custom-call.0 | solution.py:79
  406.6 1.0 fusion.32
  407.6 1.0 fusion.19
  409.4 11.7 %cholesky.70 = f32[128,128]{1,0:T(8,128)S(1)} custom-call(f32[128,128]{1,0:T(8,128)S(1)} %fusion.52), custom_call_target="Cholesky" | custom-call | tf_op jit(solution)/shard_map/jit(cholesky)/cholesky | solution.py:78
  422.5 10.3 %custom-call.10 = f32[1,128,128]{1,2,0:T(8,128)S(1)} custom-call(f32[1,128,128]{2,1,0:T(8,128)S(1)} %fusion.47), custom_call_target="InvertDiagBlocksLowerTriangular" | custom-call | tf_op jit(solution)/shard_map/triangular_solve/custom-call.0 | solution.py:79
  433.1 1.0 fusion.28
  434.6 1.0 fusion.24
  436.5 11.7 %cholesky.81 = f32[128,128]{1,0:T(8,128)S(1)} custom-call(f32[128,128]{1,0:T(8,128)S(1)} %fusion.50), custom_call_target="Cholesky" | custom-call | tf_op jit(solution)/shard_map/jit(cholesky)/cholesky | solution.py:78
  449.5 9.8 %custom-call.11 = f32[1,128,128]{1,2,0:T(8,128)S(1)} custom-call(f32[1,128,128]{2,1,0:T(8,128)S(1)} %fusion.48), custom_call_target="InvertDiagBlocksLowerTriangular" | custom-call | tf_op jit(solution)/shard_map/triangular_solve/custom-call.0 | solution.py:79
  459.7 24.6 %gather_fusion.1 = bf16[8192,128]{1,0:T(8,128)(2,1)S(1)} fusion(bf16[16384,128]{1,0:T(8,128)(2,1)} %bitcast.7, s32[8192]{0:T(1024)S(1)} %broadcast_clamp_fusion.1), kind=kCustom, calls=%fused_computation.1 | custom fusion | bytes 4227072 | tf_op jit(solution)/shard_map/jit(_take)/gather | solution.py:159
  484.3 2.7 multiply_reduce_fusion
  487.0 3.3 fusion.6
  490.4 3.3 fusion.9
  493.7 3.3 fusion.12
  497.1 4.4 fusion.78
  501.5 6.7 %convolution_subtract_fusion.1 = f32[8192,128]{1,0:T(8,128)S(1)} fusion(f32[8192,128]{1,0:T(8,128)S(1)} %fusion.9, f32[8192,128]{0,1:T(8,128)S(1)} %fusion.78, f32[384,128]{0,1:T(8,128)S(1)} %fusion.79), kind=kOutput, calls=%fused_computation.9 | convolution fusion | flops 1611661312 | bytes 12648448 | tf_op jit(solution)/shard_map/dot_general | solution.py:32
  508.2 4.6 fusion.80
  512.8 14.2 %convolution_subtract_fusion = f32[8192,128]{1,0:T(8,128)S(1)} fusion(f32[8192,128]{1,0:T(8,128)S(1)} %fusion.12, f32[8192,128]{0,1:T(8,128)S(1)} %fusion.80, f32[8192,128]{0,1:T(8,128)S(1)} %fusion.78, f32[384,128]{0,1:T(8,128)S(1)} %fusion.81, f32[384,128]{0,1:T(8,128)S(1)} %fusion.79), kind=kOutput, calls=%fused_computation.6 | convolution fusion | flops 3224403968 | bytes 17170432 | tf_op jit(solution)/shard_map/dot_general | solution.py:32
  527.1 4.1 fusion.82
  531.2 1.4 fusion
  534.0 7.0 %pad_maximum_fusion = bf16[1,1,8192,384]{2,3,1,0:T(8,128)(2,1)} fusion(bf16[1,1,8192,128]{2,3,1,0:T(8,128)(2,1)S(1)} %convert_bitcast_fusion, bf16[1,1,8192,128]{2,3,1,0:T(8,128)(2,1)S(1)} %convert_bitcast_fusion.1, bf16[1,1,8192,128]{2,3,1,0:T(8,128)(2,1)S(1)} %convert_bitcast_fusion.2), kind=kLoop, calls=%fused_computation.26 | loop fusion | flops 18874368 | bytes 12582912 | tf_op jit(solution)/shard_map/concatenate | solution.py:46
  540.9 8.6 %copy.32 = bf16[1,1,8192,384]{3,2,1,0:T(8,128)(2,1)} copy(bf16[1,1,8192,384]{2,3,1,0:T(8,128)(2,1)} %pad_maximum_fusion) | data formatting | bytes 12582912
  (70 shorter events, 13.4 us)
Async XLA Ops:
  78.0 10.2 %copy-start.4 = (s32[3]{0:T(128)S(1)}, s32[3]{0:T(128)}, u32[]{:S(2)}) copy-start(s32[3]{0:T(128)} %param.10) | copy-start | bytes 40
  78.0 12.7 %copy-start.3 = (s32[3,128]{1,0:T(4,128)S(1)}, s32[3,128]{1,0:T(4,128)}, u32[]{:S(2)}) copy-start(s32[3,128]{1,0:T(4,128)} %param.9) | copy-start | bytes 4612
  78.0 381.6 %all-to-all-start = ((bf16[16,1024,128]{2,1,0:T(8,128)(2,1)}), bf16[16,1024,128]{2,1,0:T(8,128)(2,1)}, u32[]{:S(2)}, u32[]{:S(2)}) async-start(bf16[16,1024,128]{2,1,0:T(8,128)(2,1)} %select_select_fusion), calls=%async_computation | async-start | bytes 8388608 | tf_op jit(solution)/shard_map/all_to_all | solution.py:151
  88.2 293.2 %all-reduce.3.cloned.1.call-start = ((), (), s32[]{:S(2)}) async-start(), calls=%async_computation.1 | async-start | bytes 196608 | tf_op jit(solution)/shard_map/psum | solution.py:13
  459.6 27.4 %copy-start.2 = (bf16[128,128]{1,0:T(8,128)(2,1)S(1)}, bf16[128,128]{1,0:T(8,128)(2,1)}, u32[]{:S(2)}) copy-start(bf16[128,128]{1,0:T(8,128)(2,1)} %get-tuple-element.12) | copy-start | bytes 98308
  487.0 3.3 copy-start.1
  490.4 3.3 copy-start
Sparse Core Ops, SparseCore 0:
  95.9 285.4 all-reduce.2
where the time goes:
time: 560 us; the launch traced here: 557 us
  waiting for transfers between devices  284 us (51%)
  local copies, waits for them, and re-layouts  98.4 us (18%)
  other arithmetic  94 us (17%)
  matrix products  51.8 us (9%)
  between operations  17.9 us (3%)
  starting transfers between devices  10.2 us (2%)
    psum x1, waiting for transfers between devices, from_root(): return lax.psum(block, axis)  284 us
    gather x1, local copies, waits for them, and re-layouts, per_device(): jnp.take(local_rows, take_rows, axis=0)  58.2 us
    another operation x9, other arithmetic, prepare(): factor_low = jnp.linalg.cholesky(schur_block)  37.2 us
    another operation x6, other arithmetic, prepare(): lax.linalg.triangular_solve(factor_low, identity, left_side=True, lower=T...  31.9 us
    gather x1, local copies, waits for them, and re-layouts, per_device(): points = jnp.take(flat_rows, take_index, axis=0)  24.6 us
    dot_general x3, matrix products, extend(): lax.dot_general(factors, cross_rows, (((1,), (1,)), ((), ())), precision=...  21.4 us
    dot_general x8, matrix products, affinity(): lax.dot_general(row_data, block_rows, (((1,), (1,)), ((), ())), preferred...  14.9 us
    dot_general x5, matrix products, extend(): lax.dot_general(kernel_part, inverse, (((1,), (1,)), ((), ())), precision...  14 us
  transfers between devices with their start and end apart: 2, of which 1 were waited for; matrix products, arithmetic and copies ran while one was open for 15% of the time, Pallas kernels for 0%

commit v1 on v0

--- a/solution.py
+++ b/solution.py
@@ -6,11 +6,12 @@
 PTS_DEV = 8192
 JITTER = 0.1
 HIGHEST = lax.Precision.HIGHEST
+point_fields = lambda panel, group_axis: jnp.sum(lax.all_gather(panel, group_axis), axis=0)
 
 
 def from_root(block, axis, holder):
     block = jnp.where(lax.axis_index(axis) == holder, block, jnp.zeros_like(block))
-    return lax.psum(block, axis)
+    return point_fields(block, axis)
 
 
 def squares(matrix):

time: 560 us -> 597 us (1.066)
  matrix products: 51.8 us -> 68.1 us
  other arithmetic: 94 us -> 108 us
    psum x1 -> x0, waiting for transfers between devices: 284 us -> none  [from_root(): return lax.psum(block, axis)]
    all_gather x0 -> x3, waiting for transfers between devices: none -> 177 us  [lax.all_gather(panel, group_axis)]
    all_to_all x1, waiting for transfers between devices: 0.01 us -> 106 us  [per_device(): lax.all_to_all(jnp.where(keep_mask, shaped, jnp.zeros((), local_rows.dtyp...]
    dot_general x8, matrix products: 14.9 us -> 29.9 us  [affinity(): lax.dot_general(row_data, block_rows, (((1,), (1,)), ((), ())), preferred...]
    reduce_sum x0 -> x3, other arithmetic: none -> 14.2 us  [jnp.sum(lax.all_gather(panel, group_axis), axis=0)]
  transfers between devices with their start and end apart: 2 -> 4, of which waited for: 1 -> 3; matrix products, arithmetic and copies ran while one was open for 15% -> 18% of each run, Pallas kernels for 0% -> 0%
where the time goes in v1:
time: 597 us; the launch traced here: 588 us
  waiting for transfers between devices  285 us (48%)
  other arithmetic  108 us (18%)
  local copies, waits for them, and re-layouts  98.9 us (17%)
  matrix products  68.1 us (11%)
  between operations  17.9 us (3%)
  starting transfers between devices  10.2 us (2%)
    all_gather x3, waiting for transfers between devices, lax.all_gather(panel, group_axis)  177 us
    all_to_all x1, waiting for transfers between devices, per_device(): lax.all_to_all(jnp.where(keep_mask, shaped, jnp.zeros((), local_rows.dtyp...  106 us
    gather x1, local copies, waits for them, and re-layouts, per_device(): jnp.take(local_rows, take_rows, axis=0)  58.2 us
    another operation x9, other arithmetic, prepare(): factor_low = jnp.linalg.cholesky(schur_block)  37.2 us
    another operation x6, other arithmetic, prepare(): lax.linalg.triangular_solve(factor_low, identity, left_side=True, lower=T...  31.8 us
    dot_general x8, matrix products, affinity(): lax.dot_general(row_data, block_rows, (((1,), (1,)), ((), ())), preferred...  29.9 us
    gather x1, local copies, waits for them, and re-layouts, per_device(): points = jnp.take(flat_rows, take_index, axis=0)  24.6 us
    dot_general x3, matrix products, extend(): lax.dot_general(factors, cross_rows, (((1,), (1,)), ((), ())), precision=...  21.4 us
  transfers between devices with their start and end apart: 4, of which 3 were waited for; matrix products, arithmetic and copies ran while one was open for 18% of the time, Pallas kernels for 0%

profile of v1, /device:TPU:1, one launch (start us, length us, event | category | flops | bytes accessed | tf_op | source)
XLA Modules:
  0.0 588.4 jit_solution(6224210699917319006)
XLA Ops:
  7.2 1.4 fusion.77
  12.0 3.9 gather_fusion.2
  18.2 0.9 reduce_window_sum.11
  19.1 0.7 sub.107
  23.2 58.2 %gather_fusion = bf16[16384,128]{1,0:T(8,128)(2,1)} fusion(bf16[16384,128]{1,0:T(8,128)(2,1)} %bitcast.112, s32[16384]{0:T(1024)S(1)} %broadcast_clamp_fusion), kind=kCustom, calls=%fused_computation | custom fusion | bytes 8454144 | tf_op jit(solution)/shard_map/jit(_take)/gather | solution.py:148
  81.4 7.6 %select_select_fusion = bf16[16,1024,128]{2,1,0:T(8,128)(2,1)} fusion(bf16[16,1024,128]{2,1,0:T(8,128)(2,1)} %bitcast.113, pred[16,1024]{1,0:T(8,128)(4,1)S(1)} %get-tuple-element.18, pred[16,1024]{1,0:T(8,128)(4,1)S(1)} %get-tuple-element.17), kind=kLoop, calls=%fused_computation.28 | loop fusion | flops 4194304 | bytes 8421376 | tf_op jit(solution)/shard_map/jit(_where)/select_n | solution.py:153
  89.1 10.1 %all-to-all-start = ((bf16[16,1024,128]{2,1,0:T(8,128)(2,1)}), bf16[16,1024,128]{2,1,0:T(8,128)(2,1)}, u32[]{:S(2)}, u32[]{:S(2)}) async-start(bf16[16,1024,128]{2,1,0:T(8,128)(2,1)} %select_select_fusion), calls=%async_computation | async-start | bytes 8388608 | tf_op jit(solution)/shard_map/all_to_all | solution.py:152
  100.6 105.9 %all-to-all-done = bf16[16,1024,128]{2,1,0:T(8,128)(2,1)} async-done(((bf16[16,1024,128]{2,1,0:T(8,128)(2,1)}), bf16[16,1024,128]{2,1,0:T(8,128)(2,1)}, u32[]{:S(2)}, u32[]{:S(2)}) %all-to-all-start) | async-done | bytes 4194336 | tf_op jit(solution)/shard_map/all_to_all | solution.py:152
  206.5 24.6 %gather_fusion.1 = bf16[8192,128]{1,0:T(8,128)(2,1)S(1)} fusion(bf16[16384,128]{1,0:T(8,128)(2,1)} %bitcast.7, s32[8192]{0:T(1024)S(1)} %broadcast_clamp_fusion.1), kind=kCustom, calls=%fused_computation.1 | custom fusion | bytes 4227072 | tf_op jit(solution)/shard_map/jit(_take)/gather | solution.py:160
  231.1 2.6 multiply_reduce_fusion
  233.7 4.7 reduce_sum.91
  238.4 63.4 %all-gather.9.cloned.1.call-done = bf16[32768,128]{1,0:T(8,128)(2,1)} async-done(((bf16[128,128]{1,0:T(8,128)(2,1)}), bf16[32768,128]{1,0:T(8,128)(2,1)}) %all-gather.9.cloned.1.call-update) | async-done | bytes 8388624 | tf_op jit(solution)/shard_map/all_gather | solution.py:9
  301.8 4.7 reduce_sum.92
  306.6 114.0 %all-gather.11.cloned.1.call-done = bf16[32768,128]{1,0:T(8,128)(2,1)} async-done(((bf16[128,128]{1,0:T(8,128)(2,1)}), bf16[32768,128]{1,0:T(8,128)(2,1)}) %all-gather.11.cloned.1.call-update) | async-done | bytes 8388624 | tf_op jit(solution)/shard_map/all_gather | solution.py:9
  420.5 4.7 reduce_sum.93
  425.8 9.6 %fusion.6 = f32[8192,128]{1,0:T(8,128)} fusion(bf16[128,128]{1,0:T(8,128)(2,1)S(1)} %reduce_sum.91, s32[128]{0:T(128)S(1)} %get-tuple-element.22, f32[128]{0:T(128)S(1)} %get-tuple-element.19, f32[8192]{0:T(1024)S(1)} %multiply_reduce_fusion, s32[8192]{0:T(1024)S(1)} %iota_add_fusion, bf16[8192,128]{1,0:T(8,128)(2,1)S(1)} %gather_fusion.1, ...), kind=kOutput, calls=%fused_computation.16 | convolution fusion | flops 276824064 | bytes 6398976 | tf_op jit(solution)/shard_map/dot_general | solution.py:22
  435.4 9.5 %fusion.9 = f32[8192,128]{1,0:T(8,128)} fusion(bf16[128,128]{1,0:T(8,128)(2,1)S(1)} %reduce_sum.92, s32[128]{0:T(128)S(1)} %get-tuple-element.24, f32[128]{0:T(128)S(1)} %get-tuple-element.21, f32[8192]{0:T(1024)S(1)} %multiply_reduce_fusion, s32[8192]{0:T(1024)S(1)} %iota_add_fusion, bf16[8192,128]{1,0:T(8,128)(2,1)S(1)} %gather_fusion.1, ...), kind=kOutput, calls=%fused_computation.19 | convolution fusion | flops 276824064 | bytes 6398976 | tf_op jit(solution)/shard_map/dot_general | solution.py:22
  445.1 9.8 %fusion.12 = f32[8192,128]{1,0:T(8,128)} fusion(bf16[128,128]{1,0:T(8,128)(2,1)S(1)} %reduce_sum.93, s32[128]{0:T(128)S(1)} %get-tuple-element.23, f32[128]{0:T(128)S(1)} %get-tuple-element.20, f32[8192]{0:T(1024)S(1)} %multiply_reduce_fusion, s32[8192]{0:T(1024)S(1)} %iota_add_fusion, bf16[8192,128]{1,0:T(8,128)(2,1)S(1)} %gather_fusion.1, ...), kind=kOutput, calls=%fused_computation.22 | convolution fusion | flops 276824064 | bytes 6398976 | tf_op jit(solution)/shard_map/dot_general | solution.py:22
  455.0 11.7 %cholesky.59 = f32[128,128]{1,0:T(8,128)S(1)} custom-call(f32[128,128]{1,0:T(8,128)S(1)} %fusion.54), custom_call_target="Cholesky" | custom-call | tf_op jit(solution)/shard_map/jit(cholesky)/cholesky | solution.py:79
  468.1 9.8 %custom-call.9 = f32[1,128,128]{1,2,0:T(8,128)S(1)} custom-call(f32[1,128,128]{2,1,0:T(8,128)S(1)} %fusion.46), custom_call_target="InvertDiagBlocksLowerTriangular" | custom-call | tf_op jit(solution)/shard_map/triangular_solve/custom-call.0 | solution.py:80
  479.7 11.7 %cholesky.70 = f32[128,128]{1,0:T(8,128)S(1)} custom-call(f32[128,128]{1,0:T(8,128)S(1)} %fusion.52), custom_call_target="Cholesky" | custom-call | tf_op jit(solution)/shard_map/jit(cholesky)/cholesky | solution.py:79
  492.8 10.2 %custom-call.10 = f32[1,128,128]{1,2,0:T(8,128)S(1)} custom-call(f32[1,128,128]{2,1,0:T(8,128)S(1)} %fusion.47), custom_call_target="InvertDiagBlocksLowerTriangular" | custom-call | tf_op jit(solution)/shard_map/triangular_solve/custom-call.0 | solution.py:80
  504.4 11.7 %cholesky.81 = f32[128,128]{1,0:T(8,128)S(1)} custom-call(f32[128,128]{1,0:T(8,128)S(1)} %fusion.50), custom_call_target="Cholesky" | custom-call | tf_op jit(solution)/shard_map/jit(cholesky)/cholesky | solution.py:79
  517.4 9.8 %custom-call.11 = f32[1,128,128]{1,2,0:T(8,128)S(1)} custom-call(f32[1,128,128]{2,1,0:T(8,128)S(1)} %fusion.48), custom_call_target="InvertDiagBlocksLowerTriangular" | custom-call | tf_op jit(solution)/shard_map/triangular_solve/custom-call.0 | solution.py:80
  527.6 5.9 %fusion.78 = f32[8192,128]{0,1:T(8,128)S(1)} fusion(f32[8192,128]{1,0:T(8,128)} %fusion.6, f32[128,128]{1,0:T(8,128)S(1)} %fusion.41), kind=kOutput, calls=%fused_computation.174 | convolution fusion | flops 1610612736 | bytes 8454144 | tf_op jit(solution)/shard_map/dot_general | solution.py:40
  533.5 6.7 %convolution_subtract_fusion.1 = f32[8192,128]{1,0:T(8,128)S(1)} fusion(f32[8192,128]{1,0:T(8,128)S(1)} %copy-done, f32[8192,128]{0,1:T(8,128)S(1)} %fusion.78, f32[384,128]{0,1:T(8,128)S(1)} %fusion.79), kind=kOutput, calls=%fused_computation.9 | convolution fusion | flops 1611661312 | bytes 12648448 | tf_op jit(solution)/shard_map/dot_general | solution.py:33
  540.2 4.2 fusion.80
  544.4 14.2 %convolution_subtract_fusion = f32[8192,128]{1,0:T(8,128)S(1)} fusion(f32[8192,128]{1,0:T(8,128)S(1)} %copy-done.1, f32[8192,128]{0,1:T(8,128)S(1)} %fusion.80, f32[8192,128]{0,1:T(8,128)S(1)} %fusion.78, f32[384,128]{0,1:T(8,128)S(1)} %fusion.81, f32[384,128]{0,1:T(8,128)S(1)} %fusion.79), kind=kOutput, calls=%fused_computation.6 | convolution fusion | flops 3224403968 | bytes 17170432 | tf_op jit(solution)/shard_map/dot_general | solution.py:33
  558.7 4.4 fusion.82
  563.1 1.4 fusion
  565.8 7.0 %pad_maximum_fusion = bf16[1,1,8192,384]{2,3,1,0:T(8,128)(2,1)} fusion(bf16[1,1,8192,128]{2,3,1,0:T(8,128)(2,1)S(1)} %convert_bitcast_fusion, bf16[1,1,8192,128]{2,3,1,0:T(8,128)(2,1)S(1)} %convert_bitcast_fusion.1, bf16[1,1,8192,128]{2,3,1,0:T(8,128)(2,1)S(1)} %convert_bitcast_fusion.2), kind=kLoop, calls=%fused_computation.26 | loop fusion | flops 18874368 | bytes 12582912 | tf_op jit(solution)/shard_map/concatenate | solution.py:47
  572.8 8.6 %copy.32 = bf16[1,1,8192,384]{3,2,1,0:T(8,128)(2,1)} copy(bf16[1,1,8192,384]{2,3,1,0:T(8,128)(2,1)} %pad_maximum_fusion) | data formatting | bytes 12582912
  (77 shorter events, 16.7 us)
Async XLA Ops:
  7.2 226.5 %all-gather.7.cloned.1.call-start = ((), (), s32[]{:S(2)}) async-start(), calls=%async_computation.1 | async-start | bytes 8421376 | tf_op jit(solution)/shard_map/all_gather | solution.py:9
  16.7 285.1 %all-gather.9.cloned.1.call-start = ((), (), s32[]{:S(2)}) async-start(), calls=%async_computation.2 | async-start | bytes 8421376 | tf_op jit(solution)/shard_map/all_gather | solution.py:9
  17.5 403.0 %all-gather.11.cloned.1.call-start = ((), (), s32[]{:S(2)}) async-start(), calls=%async_computation.3 | async-start | bytes 8421376 | tf_op jit(solution)/shard_map/all_gather | solution.py:9
  89.1 10.1 %copy-start.3 = (s32[3]{0:T(128)S(1)}, s32[3]{0:T(128)}, u32[]{:S(2)}) copy-start(s32[3]{0:T(128)} %param.10) | copy-start | bytes 40
  89.1 11.2 %copy-start.2 = (s32[3,128]{1,0:T(4,128)S(1)}, s32[3,128]{1,0:T(4,128)}, u32[]{:S(2)}) copy-start(s32[3,128]{1,0:T(4,128)} %param.9) | copy-start | bytes 4612
  89.1 117.4 %all-to-all-start = ((bf16[16,1024,128]{2,1,0:T(8,128)(2,1)}), bf16[16,1024,128]{2,1,0:T(8,128)(2,1)}, u32[]{:S(2)}, u32[]{:S(2)}) async-start(bf16[16,1024,128]{2,1,0:T(8,128)(2,1)} %select_select_fusion), calls=%async_computation | async-start | bytes 8388608 | tf_op jit(solution)/shard_map/all_to_all | solution.py:152
  527.6 5.9 %copy-start = (f32[8192,128]{1,0:T(8,128)S(1)}, f32[8192,128]{1,0:T(8,128)}, u32[]{:S(2)}) copy-start(f32[8192,128]{1,0:T(8,128)} %fusion.9) | copy-start | bytes 12582916
  540.2 4.2 copy-start.1
Sparse Core Ops, SparseCore 0:
  16.9 156.3 all-gather.6
  176.9 124.8 all-gather.8
  305.5 114.9 all-gather.10
